TPU v7x, 512 devices: a whole 4x4x16 slice. The times are simulated.
512 devices in a mesh: blk: 128 (over z, x, core), rhs: 4 (over y).
Axes of the slice: x: 4, y: 4, z: 16, core: 2. Of those that a mesh axis runs over, the one named last changes fastest.
Arguments:
- right_sides: bfloat16 [4, 4, 128, 320, 256], P(None, None, 'blk', 'rhs'), may hold values from -6 to 6
- inverse_blocks: bfloat16 [4, 4, 128, 256, 256], P(None, None, 'blk', 'rhs'), as said below
- lower_blocks: bfloat16 [3, 4, 128, 6, 256, 256], P(None, None, 'blk', None, 'rhs'), may hold values from -0.21875 to 0.21875
- row_counts: int32 [3, 4, 128], P(None, None, 'blk'), may hold values from 1 to 6, as said below
Outputs:
- solution: bfloat16 [4, 4, 128, 320, 256], P(None, None, 'blk', 'rhs')
Inputs may be any that keep to these rules, and one draw needn't show every extreme that they name: `row_counts`: in every level some supernode column has 6 row blocks. Every block of inverse_blocks is lower triangular: its entries above the diagonal are zero and its diagonal entries are positive.
All inputs are finite; a program needn't handle non-finite values.
Results may differ from a plain program's by a relative error of at most 0.0061.
Values may be sent and summed in bfloat16 or wider, within the bound.
No kernel may reach another device: no remote copies, remote signals or barrier semaphores. Data moves between devices by JAX's collectives and lax.ppermute only.
A program may use at most 64 MiB of HBM per device.

v0:
```python
import jax
import jax.numpy as jnp
from jax import lax
from jax.sharding import PartitionSpec as P


def passed_along(shard, axis, by):
    count = lax.axis_size(axis)
    return lax.ppermute(shard, axis, [(i, (i + by) % count) for i in range(count)])


def slot_offset(slot):
    return (slot // 2 + 1) * (1 if slot % 2 == 0 else -1)


def local(right_sides, inverse_blocks, lower_blocks, row_counts):
    levels_total = right_sides.shape[0]
    reach_slots = lower_blocks.shape[3]
    incoming = jnp.zeros(right_sides.shape[1:], jnp.float32)
    solved_levels = []
    for level in range(levels_total):
        rest_block = (right_sides[level].astype(jnp.float32) - incoming).astype(jnp.bfloat16)
        solved_wide = jnp.einsum(
            "kprj,kpij->kpri",
            rest_block,
            lax.all_gather(inverse_blocks[level], "rhs", axis=2, tiled=True),
            preferred_element_type=jnp.float32,
        )
        solved = solved_wide.astype(jnp.bfloat16)
        solved_levels.append(solved)
        if level + 1 < levels_total:
            updates = jnp.einsum(
                "kpsij,kprj->skpri",
                lax.all_gather(lower_blocks[level], "rhs", axis=3, tiled=True),
                solved,
                preferred_element_type=jnp.float32,
            )
            slot_index = lax.broadcasted_iota(jnp.int32, (reach_slots,) + row_counts.shape[1:], 0)
            active = (slot_index < row_counts[level][None]).astype(jnp.float32)
            updates = updates * active[..., None, None]
            incoming = jnp.zeros(right_sides.shape[1:], jnp.float32)
            for slot in range(reach_slots):
                incoming = incoming + passed_along(updates[slot], "blk", slot_offset(slot))
    return jnp.stack(solved_levels)


def solution(mesh):
    return jax.shard_map(
        local,
        mesh=mesh,
        in_specs=(
            P(None, None, "blk", "rhs", None),
            P(None, None, "blk", "rhs", None),
            P(None, None, "blk", None, "rhs", None),
            P(None, None, "blk"),
        ),
        out_specs=P(None, None, "blk", "rhs", None),
        check_vma=False,
    )
```

profile of v0, /device:TPU:16, one launch (start us, length us, event | category | flops | bytes accessed | tf_op | source)
XLA Modules:
  0.0 219.2 jit_solution(11464316395482875335)
XLA Ops:
  6.5 3.1 %fusion.32 = (bf16[1,4,1,6,64,256]{5,4,3,1,2,0:T(8,128)(2,1)}, bf16[1,4,1,6,64,256]{5,4,3,1,2,0:T(8,128)(2,1)}, bf16[1,4,1,6,64,256]{5,4,3,1,2,0:T(8,128)(2,1)}) fusion(bf16[3,4,1,6,64,256]{5,4,3,1,2,0:T(8,128)(2,1)} %bitcast.174), kind=kLoop, calls=%fused_computation.62 | loop fusion | bytes 4718592 | tf_op jit(solution)/shard_map/slice | solution.py:34
  9.6 0.0 all-gather.11.cloned.1.call-update
  9.6 0.0 all-gather.13.cloned.1.call-start
  9.7 0.7 all-gather.13.cloned.1.call-update
  10.4 0.0 all-gather.15.cloned.1.call-start
  10.4 0.7 all-gather.15.cloned.1.call-update
  11.2 16.4 %all-gather = bf16[1,4,1,256,256]{4,3,1,2,0:T(8,128)(2,1)S(1)} all-gather(bf16[1,4,1,64,256]{4,3,1,2,0:T(8,128)(2,1)S(1)} %get-tuple-element.26), channel_id=2, replica_groups=mesh['blk'=128,'rhs'=4] {'rhs'}, dimensions={3}, use_global_device_ids=true | all-gather | bytes 655360 | tf_op jit(solution)/shard_map/all_gather | solution.py:26
  27.6 0.1 fusion.29
  27.7 0.3 convolution_convert_fusion.3
  27.9 32.3 %all-gather.11.cloned.1.call-done = bf16[1,4,1,6,256,256]{5,4,3,1,2,0:T(8,128)(2,1)} async-done(((bf16[1,4,1,6,64,256]{5,4,3,1,2,0:T(8,128)(2,1)}), bf16[1,4,1,6,256,256]{5,4,3,1,2,0:T(8,128)(2,1)}) %all-gather.11.cloned.1.call-update) | async-done | bytes 3145744 | tf_op jit(solution)/shard_map/all_gather | solution.py:34
  60.2 3.0 %bitcast_multiply_fusion.2 = f32[6,4,1,80,256]{4,3,0,1,2:T(8,128)S(1)} fusion(bf16[1,4,1,6,256,256]{5,4,3,1,2,0:T(8,128)(2,1)} %all-gather.11.cloned.1.call-done, f32[6,4]{0,1:T(4,128)S(1)} %fusion.29, bf16[4,80,256]{2,1,0:T(8,128)(2,1)S(1)} %convolution_convert_fusion.3), kind=kOutput, calls=%fused_computation.8 | convolution fusion | flops 252149760 | bytes 5275744 | tf_op jit(solution)/shard_map/kpsij,kprj->skpri/dot_general | solution.py:32
  63.2 0.1 slice_bitcast_fusion.16
  63.3 1.9 collective-permute-start
  65.2 7.3 %collective-permute-start.1 = (f32[4,1,80,256]{3,2,0,1:T(8,128)S(1)}, f32[4,1,80,256]{3,2,0,1:T(8,128)S(1)}, u32[]{:S(2)}, u32[]{:S(2)}) collective-permute-start(f32[4,1,80,256]{3,2,0,1:T(8,128)S(1)} %get-tuple-element.20), channel_id=1, source_target_pairs={{0,508},{4,0},{8,4},{12,8},{16,12},{20,16},{24,20},{28,24},{32,28}... | collective-permute-start | bytes 983048 | tf_op jit(solution)/shard_map/ppermute | solution.py:9
  72.5 1.9 collective-permute-start.2
  74.5 7.2 %collective-permute-start.3 = (f32[4,1,80,256]{3,2,0,1:T(8,128)S(1)}, f32[4,1,80,256]{3,2,0,1:T(8,128)S(1)}, u32[]{:S(2)}, u32[]{:S(2)}) collective-permute-start(f32[4,1,80,256]{3,2,0,1:T(8,128)S(1)} %get-tuple-element.21), channel_id=1, source_target_pairs={{0,504},{4,508},{8,0},{12,4},{16,8},{20,12},{24,16},{28,20},{32,24... | collective-permute-start | bytes 983048 | tf_op jit(solution)/shard_map/ppermute | solution.py:9
  81.7 1.9 collective-permute-start.4
  83.6 0.0 collective-permute-done
  83.7 7.3 %collective-permute-start.5 = (f32[4,1,80,256]{3,2,0,1:T(8,128)S(1)}, f32[4,1,80,256]{3,2,0,1:T(8,128)S(1)}, u32[]{:S(2)}, u32[]{:S(2)}) collective-permute-start(f32[4,1,80,256]{3,2,0,1:T(8,128)S(1)} %get-tuple-element.24), channel_id=1, source_target_pairs={{0,500},{4,504},{8,508},{12,0},{16,4},{20,8},{24,12},{28,16},{32,2... | collective-permute-start | bytes 983048 | tf_op jit(solution)/shard_map/ppermute | solution.py:9
  90.9 15.2 %all-gather.2 = bf16[1,4,1,256,256]{4,3,1,2,0:T(8,128)(2,1)S(1)} all-gather(bf16[1,4,1,64,256]{4,3,1,2,0:T(8,128)(2,1)S(1)} %get-tuple-element.29), channel_id=4, replica_groups=mesh['blk'=128,'rhs'=4] {'rhs'}, dimensions={3}, use_global_device_ids=true | all-gather | bytes 655360 | tf_op jit(solution)/shard_map/all_gather | solution.py:26
  106.1 0.1 fusion.30
  106.2 0.0 collective-permute-done.1
  106.2 0.3 convolution_convert_fusion.2
  106.5 7.4 %all-gather.13.cloned.1.call-done = bf16[1,4,1,6,256,256]{5,4,3,1,2,0:T(8,128)(2,1)} async-done(((bf16[1,4,1,6,64,256]{5,4,3,1,2,0:T(8,128)(2,1)}), bf16[1,4,1,6,256,256]{5,4,3,1,2,0:T(8,128)(2,1)}) %all-gather.13.cloned.1.call-update) | async-done | bytes 3145744 | tf_op jit(solution)/shard_map/all_gather | solution.py:34
  113.9 3.0 %bitcast_multiply_fusion.1 = f32[6,4,1,80,256]{4,3,0,1,2:T(8,128)S(1)} fusion(bf16[1,4,1,6,256,256]{5,4,3,1,2,0:T(8,128)(2,1)} %all-gather.13.cloned.1.call-done, f32[6,4]{0,1:T(4,128)S(1)} %fusion.30, bf16[4,80,256]{2,1,0:T(8,128)(2,1)S(1)} %convolution_convert_fusion.2), kind=kOutput, calls=%fused_computation.7 | convolution fusion | flops 252149760 | bytes 5275744 | tf_op jit(solution)/shard_map/kpsij,kprj->skpri/dot_general | solution.py:32
  116.9 0.1 slice_bitcast_fusion.10
  117.0 2.7 %collective-permute-start.10 = (f32[4,1,80,256]{3,2,0,1:T(8,128)S(1)}, f32[4,1,80,256]{3,2,0,1:T(8,128)S(1)}, u32[]{:S(2)}, u32[]{:S(2)}) collective-permute-start(f32[4,1,80,256]{3,2,0,1:T(8,128)S(1)} %get-tuple-element.19), channel_id=1, source_target_pairs={{0,12},{4,16},{8,20},{12,24},{16,28},{20,32},{24,36},{28,40},{32,4... | collective-permute-start | bytes 983048 | tf_op jit(solution)/shard_map/ppermute | solution.py:9
  119.7 6.9 %collective-permute-start.11 = (f32[4,1,80,256]{3,2,0,1:T(8,128)S(1)}, f32[4,1,80,256]{3,2,0,1:T(8,128)S(1)}, u32[]{:S(2)}, u32[]{:S(2)}) collective-permute-start(f32[4,1,80,256]{3,2,0,1:T(8,128)S(1)} %get-tuple-element.18), channel_id=1, source_target_pairs={{0,500},{4,504},{8,508},{12,0},{16,4},{20,8},{24,12},{28,16},{32,2... | collective-permute-start | bytes 983048 | tf_op jit(solution)/shard_map/ppermute | solution.py:9
  126.6 2.5 %collective-permute-start.6 = (f32[4,1,80,256]{3,2,0,1:T(8,128)S(1)}, f32[4,1,80,256]{3,2,0,1:T(8,128)S(1)}, u32[]{:S(2)}, u32[]{:S(2)}) collective-permute-start(f32[4,1,80,256]{3,2,0,1:T(8,128)S(1)} %get-tuple-element.17), channel_id=1, source_target_pairs={{0,4},{4,8},{8,12},{12,16},{16,20},{20,24},{24,28},{28,32},{32,36}... | collective-permute-start | bytes 983048 | tf_op jit(solution)/shard_map/ppermute | solution.py:9
  129.1 6.4 %collective-permute-start.7 = (f32[4,1,80,256]{3,2,0,1:T(8,128)S(1)}, f32[4,1,80,256]{3,2,0,1:T(8,128)S(1)}, u32[]{:S(2)}, u32[]{:S(2)}) collective-permute-start(f32[4,1,80,256]{3,2,0,1:T(8,128)S(1)} %get-tuple-element.14), channel_id=1, source_target_pairs={{0,508},{4,0},{8,4},{12,8},{16,12},{20,16},{24,20},{28,24},{32,28}... | collective-permute-start | bytes 983048 | tf_op jit(solution)/shard_map/ppermute | solution.py:9
  135.5 1.9 collective-permute-start.8
  137.4 0.0 collective-permute-done.10
  137.4 7.2 %collective-permute-start.9 = (f32[4,1,80,256]{3,2,0,1:T(8,128)S(1)}, f32[4,1,80,256]{3,2,0,1:T(8,128)S(1)}, u32[]{:S(2)}, u32[]{:S(2)}) collective-permute-start(f32[4,1,80,256]{3,2,0,1:T(8,128)S(1)} %get-tuple-element.15), channel_id=1, source_target_pairs={{0,504},{4,508},{8,0},{12,4},{16,8},{20,12},{24,16},{28,20},{32,24... | collective-permute-start | bytes 983048 | tf_op jit(solution)/shard_map/ppermute | solution.py:9
  144.7 15.1 %all-gather.4 = bf16[1,4,1,256,256]{4,3,1,2,0:T(8,128)(2,1)S(1)} all-gather(bf16[1,4,1,64,256]{4,3,1,2,0:T(8,128)(2,1)S(1)} %get-tuple-element.28), channel_id=6, replica_groups=mesh['blk'=128,'rhs'=4] {'rhs'}, dimensions={3}, use_global_device_ids=true | all-gather | bytes 655360 | tf_op jit(solution)/shard_map/all_gather | solution.py:26
  159.8 0.1 fusion.31
  159.9 0.3 convolution_convert_fusion.1
  160.2 7.5 %all-gather.15.cloned.1.call-done = bf16[1,4,1,6,256,256]{5,4,3,1,2,0:T(8,128)(2,1)} async-done(((bf16[1,4,1,6,64,256]{5,4,3,1,2,0:T(8,128)(2,1)}), bf16[1,4,1,6,256,256]{5,4,3,1,2,0:T(8,128)(2,1)}) %all-gather.15.cloned.1.call-update) | async-done | bytes 3145744 | tf_op jit(solution)/shard_map/all_gather | solution.py:34
  167.7 3.0 %bitcast_multiply_fusion = f32[6,4,1,80,256]{4,3,0,1,2:T(8,128)S(1)} fusion(bf16[1,4,1,6,256,256]{5,4,3,1,2,0:T(8,128)(2,1)} %all-gather.15.cloned.1.call-done, f32[6,4]{0,1:T(4,128)S(1)} %fusion.31, bf16[4,80,256]{2,1,0:T(8,128)(2,1)S(1)} %convolution_convert_fusion.1), kind=kOutput, calls=%fused_computation.6 | convolution fusion | flops 252149760 | bytes 5275744 | tf_op jit(solution)/shard_map/kpsij,kprj->skpri/dot_general | solution.py:32
  170.7 0.1 slice_bitcast_fusion.4
  170.8 1.9 collective-permute-start.12
  172.7 7.4 %collective-permute-start.13 = (f32[4,1,80,256]{3,2,0,1:T(8,128)S(1)}, f32[4,1,80,256]{3,2,0,1:T(8,128)S(1)}, u32[]{:S(2)}, u32[]{:S(2)}) collective-permute-start(f32[4,1,80,256]{3,2,0,1:T(8,128)S(1)} %get-tuple-element.8), channel_id=1, source_target_pairs={{0,508},{4,0},{8,4},{12,8},{16,12},{20,16},{24,20},{28,24},{32,28}... | collective-permute-start | bytes 983048 | tf_op jit(solution)/shard_map/ppermute | solution.py:9
  180.1 1.9 collective-permute-start.14
  182.0 7.2 %collective-permute-start.15 = (f32[4,1,80,256]{3,2,0,1:T(8,128)S(1)}, f32[4,1,80,256]{3,2,0,1:T(8,128)S(1)}, u32[]{:S(2)}, u32[]{:S(2)}) collective-permute-start(f32[4,1,80,256]{3,2,0,1:T(8,128)S(1)} %get-tuple-element.9), channel_id=1, source_target_pairs={{0,504},{4,508},{8,0},{12,4},{16,8},{20,12},{24,16},{28,20},{32,24... | collective-permute-start | bytes 983048 | tf_op jit(solution)/shard_map/ppermute | solution.py:9
  189.3 1.9 collective-permute-start.16
  191.2 7.3 %collective-permute-start.17 = (f32[4,1,80,256]{3,2,0,1:T(8,128)S(1)}, f32[4,1,80,256]{3,2,0,1:T(8,128)S(1)}, u32[]{:S(2)}, u32[]{:S(2)}) collective-permute-start(f32[4,1,80,256]{3,2,0,1:T(8,128)S(1)} %get-tuple-element.12), channel_id=1, source_target_pairs={{0,500},{4,504},{8,508},{12,0},{16,4},{20,8},{24,12},{28,16},{32,2... | collective-permute-start | bytes 983048 | tf_op jit(solution)/shard_map/ppermute | solution.py:9
  198.5 12.9 %all-gather.6 = bf16[1,4,1,256,256]{4,3,1,2,0:T(8,128)(2,1)S(1)} all-gather(bf16[1,4,1,64,256]{4,3,1,2,0:T(8,128)(2,1)S(1)} %get-tuple-element.27), channel_id=8, replica_groups=mesh['blk'=128,'rhs'=4] {'rhs'}, dimensions={3}, use_global_device_ids=true | all-gather | bytes 655360 | tf_op jit(solution)/shard_map/all_gather | solution.py:26
  211.4 0.3 fusion.12
  211.7 0.9 maximum_bitcast_fusion
  (24 shorter events, 0.1 us)
Async XLA Ops:
  6.5 53.7 %all-gather.11.cloned.1.call-start = ((), (), s32[]{:S(2)}) async-start(), calls=%async_computation | async-start | bytes 3932160 | tf_op jit(solution)/shard_map/all_gather | solution.py:34
  9.6 1.5 copy-start.1
  9.6 18.0 %copy-start.2 = (s32[3,4,1]{1,2,0:T(1,128)S(1)}, s32[3,4,1]{1,2,0:T(1,128)}, u32[]{:S(2)}) copy-start(s32[3,4,1]{1,2,0:T(1,128)} %param.7) | copy-start | bytes 148
  9.6 18.1 %copy-start = (bf16[4,4,1,80,256]{4,3,2,1,0:T(8,128)(2,1)S(1)}, bf16[4,4,1,80,256]{4,3,2,1,0:T(8,128)(2,1)}, u32[]{:S(2)}) copy-start(bf16[4,4,1,80,256]{4,3,2,1,0:T(8,128)(2,1)} %param.4) | copy-start | bytes 1966084
  9.6 104.3 %all-gather.13.cloned.1.call-start = ((), (), s32[]{:S(2)}) async-start(), calls=%async_computation.1 | async-start | bytes 3932160 | tf_op jit(solution)/shard_map/all_gather | solution.py:34
  10.4 157.3 %all-gather.15.cloned.1.call-start = ((), (), s32[]{:S(2)}) async-start(), calls=%async_computation.2 | async-start | bytes 3932160 | tf_op jit(solution)/shard_map/all_gather | solution.py:34
  63.3 20.4 %collective-permute-start = (f32[4,1,80,256]{3,2,0,1:T(8,128)S(1)}, f32[4,1,80,256]{3,2,0,1:T(8,128)S(1)}, u32[]{:S(2)}, u32[]{:S(2)}) collective-permute-start(f32[4,1,80,256]{3,2,0,1:T(8,128)S(1)} %get-tuple-element.23), channel_id=1, source_target_pairs={{0,4},{4,8},{8,12},{12,16},{16,20},{20,24},{24,28},{28,32},{32,36}... | collective-permute-start | bytes 983048 | tf_op jit(solution)/shard_map/ppermute | solution.py:9
  65.2 41.0 %collective-permute-start.1 = (f32[4,1,80,256]{3,2,0,1:T(8,128)S(1)}, f32[4,1,80,256]{3,2,0,1:T(8,128)S(1)}, u32[]{:S(2)}, u32[]{:S(2)}) collective-permute-start(f32[4,1,80,256]{3,2,0,1:T(8,128)S(1)} %get-tuple-element.20), channel_id=1, source_target_pairs={{0,508},{4,0},{8,4},{12,8},{16,12},{20,16},{24,20},{28,24},{32,28}... | collective-permute-start | bytes 983048 | tf_op jit(solution)/shard_map/ppermute | solution.py:9
  72.5 33.7 %collective-permute-start.2 = (f32[4,1,80,256]{3,2,0,1:T(8,128)S(1)}, f32[4,1,80,256]{3,2,0,1:T(8,128)S(1)}, u32[]{:S(2)}, u32[]{:S(2)}) collective-permute-start(f32[4,1,80,256]{3,2,0,1:T(8,128)S(1)} %get-tuple-element.22), channel_id=1, source_target_pairs={{0,8},{4,12},{8,16},{12,20},{16,24},{20,28},{24,32},{28,36},{32,40... | collective-permute-start | bytes 983048 | tf_op jit(solution)/shard_map/ppermute | solution.py:9
  74.5 31.7 %collective-permute-start.3 = (f32[4,1,80,256]{3,2,0,1:T(8,128)S(1)}, f32[4,1,80,256]{3,2,0,1:T(8,128)S(1)}, u32[]{:S(2)}, u32[]{:S(2)}) collective-permute-start(f32[4,1,80,256]{3,2,0,1:T(8,128)S(1)} %get-tuple-element.21), channel_id=1, source_target_pairs={{0,504},{4,508},{8,0},{12,4},{16,8},{20,12},{24,16},{28,20},{32,24... | collective-permute-start | bytes 983048 | tf_op jit(solution)/shard_map/ppermute | solution.py:9
  81.7 24.5 %collective-permute-start.4 = (f32[4,1,80,256]{3,2,0,1:T(8,128)S(1)}, f32[4,1,80,256]{3,2,0,1:T(8,128)S(1)}, u32[]{:S(2)}, u32[]{:S(2)}) collective-permute-start(f32[4,1,80,256]{3,2,0,1:T(8,128)S(1)} %get-tuple-element.25), channel_id=1, source_target_pairs={{0,12},{4,16},{8,20},{12,24},{16,28},{20,32},{24,36},{28,40},{32,4... | collective-permute-start | bytes 983048 | tf_op jit(solution)/shard_map/ppermute | solution.py:9
  83.7 22.6 %collective-permute-start.5 = (f32[4,1,80,256]{3,2,0,1:T(8,128)S(1)}, f32[4,1,80,256]{3,2,0,1:T(8,128)S(1)}, u32[]{:S(2)}, u32[]{:S(2)}) collective-permute-start(f32[4,1,80,256]{3,2,0,1:T(8,128)S(1)} %get-tuple-element.24), channel_id=1, source_target_pairs={{0,500},{4,504},{8,508},{12,0},{16,4},{20,8},{24,12},{28,16},{32,2... | collective-permute-start | bytes 983048 | tf_op jit(solution)/shard_map/ppermute | solution.py:9
  117.0 20.4 %collective-permute-start.10 = (f32[4,1,80,256]{3,2,0,1:T(8,128)S(1)}, f32[4,1,80,256]{3,2,0,1:T(8,128)S(1)}, u32[]{:S(2)}, u32[]{:S(2)}) collective-permute-start(f32[4,1,80,256]{3,2,0,1:T(8,128)S(1)} %get-tuple-element.19), channel_id=1, source_target_pairs={{0,12},{4,16},{8,20},{12,24},{16,28},{20,32},{24,36},{28,40},{32,4... | collective-permute-start | bytes 983048 | tf_op jit(solution)/shard_map/ppermute | solution.py:9
  119.7 40.2 %collective-permute-start.11 = (f32[4,1,80,256]{3,2,0,1:T(8,128)S(1)}, f32[4,1,80,256]{3,2,0,1:T(8,128)S(1)}, u32[]{:S(2)}, u32[]{:S(2)}) collective-permute-start(f32[4,1,80,256]{3,2,0,1:T(8,128)S(1)} %get-tuple-element.18), channel_id=1, source_target_pairs={{0,500},{4,504},{8,508},{12,0},{16,4},{20,8},{24,12},{28,16},{32,2... | collective-permute-start | bytes 983048 | tf_op jit(solution)/shard_map/ppermute | solution.py:9
  126.6 33.3 %collective-permute-start.6 = (f32[4,1,80,256]{3,2,0,1:T(8,128)S(1)}, f32[4,1,80,256]{3,2,0,1:T(8,128)S(1)}, u32[]{:S(2)}, u32[]{:S(2)}) collective-permute-start(f32[4,1,80,256]{3,2,0,1:T(8,128)S(1)} %get-tuple-element.17), channel_id=1, source_target_pairs={{0,4},{4,8},{8,12},{12,16},{16,20},{20,24},{24,28},{28,32},{32,36}... | collective-permute-start | bytes 983048 | tf_op jit(solution)/shard_map/ppermute | solution.py:9
  129.1 30.8 %collective-permute-start.7 = (f32[4,1,80,256]{3,2,0,1:T(8,128)S(1)}, f32[4,1,80,256]{3,2,0,1:T(8,128)S(1)}, u32[]{:S(2)}, u32[]{:S(2)}) collective-permute-start(f32[4,1,80,256]{3,2,0,1:T(8,128)S(1)} %get-tuple-element.14), channel_id=1, source_target_pairs={{0,508},{4,0},{8,4},{12,8},{16,12},{20,16},{24,20},{28,24},{32,28}... | collective-permute-start | bytes 983048 | tf_op jit(solution)/shard_map/ppermute | solution.py:9
  135.5 24.4 %collective-permute-start.8 = (f32[4,1,80,256]{3,2,0,1:T(8,128)S(1)}, f32[4,1,80,256]{3,2,0,1:T(8,128)S(1)}, u32[]{:S(2)}, u32[]{:S(2)}) collective-permute-start(f32[4,1,80,256]{3,2,0,1:T(8,128)S(1)} %get-tuple-element.16), channel_id=1, source_target_pairs={{0,8},{4,12},{8,16},{12,20},{16,24},{20,28},{24,32},{28,36},{32,40... | collective-permute-start | bytes 983048 | tf_op jit(solution)/shard_map/ppermute | solution.py:9
  137.4 22.5 %collective-permute-start.9 = (f32[4,1,80,256]{3,2,0,1:T(8,128)S(1)}, f32[4,1,80,256]{3,2,0,1:T(8,128)S(1)}, u32[]{:S(2)}, u32[]{:S(2)}) collective-permute-start(f32[4,1,80,256]{3,2,0,1:T(8,128)S(1)} %get-tuple-element.15), channel_id=1, source_target_pairs={{0,504},{4,508},{8,0},{12,4},{16,8},{20,12},{24,16},{28,20},{32,24... | collective-permute-start | bytes 983048 | tf_op jit(solution)/shard_map/ppermute | solution.py:9
  170.8 20.4 %collective-permute-start.12 = (f32[4,1,80,256]{3,2,0,1:T(8,128)S(1)}, f32[4,1,80,256]{3,2,0,1:T(8,128)S(1)}, u32[]{:S(2)}, u32[]{:S(2)}) collective-permute-start(f32[4,1,80,256]{3,2,0,1:T(8,128)S(1)} %get-tuple-element.11), channel_id=1, source_target_pairs={{0,4},{4,8},{8,12},{12,16},{16,20},{20,24},{24,28},{28,32},{32,36}... | collective-permute-start | bytes 983048 | tf_op jit(solution)/shard_map/ppermute | solution.py:9
  172.7 38.7 %collective-permute-start.13 = (f32[4,1,80,256]{3,2,0,1:T(8,128)S(1)}, f32[4,1,80,256]{3,2,0,1:T(8,128)S(1)}, u32[]{:S(2)}, u32[]{:S(2)}) collective-permute-start(f32[4,1,80,256]{3,2,0,1:T(8,128)S(1)} %get-tuple-element.8), channel_id=1, source_target_pairs={{0,508},{4,0},{8,4},{12,8},{16,12},{20,16},{24,20},{28,24},{32,28}... | collective-permute-start | bytes 983048 | tf_op jit(solution)/shard_map/ppermute | solution.py:9
  180.1 31.3 %collective-permute-start.14 = (f32[4,1,80,256]{3,2,0,1:T(8,128)S(1)}, f32[4,1,80,256]{3,2,0,1:T(8,128)S(1)}, u32[]{:S(2)}, u32[]{:S(2)}) collective-permute-start(f32[4,1,80,256]{3,2,0,1:T(8,128)S(1)} %get-tuple-element.10), channel_id=1, source_target_pairs={{0,8},{4,12},{8,16},{12,20},{16,24},{20,28},{24,32},{28,36},{32,40... | collective-permute-start | bytes 983048 | tf_op jit(solution)/shard_map/ppermute | solution.py:9
  182.0 29.4 %collective-permute-start.15 = (f32[4,1,80,256]{3,2,0,1:T(8,128)S(1)}, f32[4,1,80,256]{3,2,0,1:T(8,128)S(1)}, u32[]{:S(2)}, u32[]{:S(2)}) collective-permute-start(f32[4,1,80,256]{3,2,0,1:T(8,128)S(1)} %get-tuple-element.9), channel_id=1, source_target_pairs={{0,504},{4,508},{8,0},{12,4},{16,8},{20,12},{24,16},{28,20},{32,24... | collective-permute-start | bytes 983048 | tf_op jit(solution)/shard_map/ppermute | solution.py:9
  189.3 22.1 %collective-permute-start.16 = (f32[4,1,80,256]{3,2,0,1:T(8,128)S(1)}, f32[4,1,80,256]{3,2,0,1:T(8,128)S(1)}, u32[]{:S(2)}, u32[]{:S(2)}) collective-permute-start(f32[4,1,80,256]{3,2,0,1:T(8,128)S(1)} %get-tuple-element.13), channel_id=1, source_target_pairs={{0,12},{4,16},{8,20},{12,24},{16,28},{20,32},{24,36},{28,40},{32,4... | collective-permute-start | bytes 983048 | tf_op jit(solution)/shard_map/ppermute | solution.py:9
  191.2 20.2 %collective-permute-start.17 = (f32[4,1,80,256]{3,2,0,1:T(8,128)S(1)}, f32[4,1,80,256]{3,2,0,1:T(8,128)S(1)}, u32[]{:S(2)}, u32[]{:S(2)}) collective-permute-start(f32[4,1,80,256]{3,2,0,1:T(8,128)S(1)} %get-tuple-element.12), channel_id=1, source_target_pairs={{0,500},{4,504},{8,508},{12,0},{16,4},{20,8},{24,12},{28,16},{32,2... | collective-permute-start | bytes 983048 | tf_op jit(solution)/shard_map/ppermute | solution.py:9
Sparse Core Ops, SparseCore 0:
  9.7 50.4 all-gather.10
  62.3 51.5 all-gather.12
  116.0 51.6 all-gather.14
where the time goes:
time: 220 us; the launch traced here: 219 us
  starting transfers between devices  82.9 us (38%)
  blocking collectives  59.7 us (27%)
  waiting for transfers between devices  48.6 us (22%)
  between operations  13.4 us (6%)
  matrix products  10 us (5%)
  local copies, waits for them, and re-layouts  3.5 us (2%)
    ppermute x18, starting transfers between devices, passed_along(): lax.ppermute(shard, axis, [(i, (i + by) % count) for i in range(count)])  82.8 us
    all_gather x4, blocking collectives, local(): lax.all_gather(inverse_blocks[level], 'rhs', axis=2, tiled=True)  59.7 us
    all_gather x3, waiting for transfers between devices, local(): lax.all_gather(lower_blocks[level], 'rhs', axis=3, tiled=True)  47.1 us
    dot_general x3, matrix products, local(): jnp.einsum('kpsij,kprj->skpri', lax.all_gather(lower_blocks[level], 'rhs'...  8.86 us
  transfers between devices with their start and end apart: 21, of which 3 were waited for; matrix products, arithmetic and copies ran while one was open for 3% of the time, Pallas kernels for 0%

commit v1 on v0

v1 whole, which is shorter than its diff:
```python
import jax
import jax.numpy as jnp
from jax import lax
from jax.sharding import PartitionSpec as P

AXES = ("blk", "rhs")
BATCHES = ((0,), (1,), (2, 3))


def local(n_blk, right_sides, inverse_blocks, lower_blocks, row_counts):
    levels = right_sides.shape[0]
    chunk, block = inverse_blocks.shape[3], inverse_blocks.shape[4]
    part = right_sides.shape[3]
    core = lax.axis_index("blk") % 2
    me = lax.axis_index("rhs")
    first = jnp.where(core == 0, 1, 3)
    second = 4 - first
    bf16, f32 = jnp.bfloat16, jnp.float32

    def routed(x, to):
        pairs = []
        for b in range(n_blk):
            for r in range(4):
                nb, nr = to(b, r)
                pairs.append((b * 4 + r, (nb % n_blk) * 4 + nr))
        return lax.ppermute(x, AXES, pairs)

    def to_first(x):
        return routed(x, lambda b, r: (b, r ^ (1 if b % 2 == 0 else 3)))

    def to_second(x):
        return routed(x, lambda b, r: (b, r ^ (3 if b % 2 == 0 else 1)))

    def to_core(x):
        return routed(x, lambda b, r: (b ^ 1, r))

    def to_next(x, chips):
        return routed(x, lambda b, r: (b + 2 * chips if b % 2 == 0 else b - 2 * chips, r))

    def exchanged(pick):
        got1 = to_first(jnp.stack([pick(first), pick(2)]))
        got2 = to_second(jnp.stack([pick(second), got1[1]]))
        one = jnp.where(core == 0, got1[0], got2[0])
        three = jnp.where(core == 0, got2[0], got1[0])
        return jnp.stack([pick(0), one, got2[1], three])

    def in_order(x):
        x = jnp.where(me & 1, jnp.stack([x[1], x[0], x[3], x[2]]), x)
        return jnp.where(me & 2, jnp.concatenate([x[2:], x[:2]]), x)

    def dyn(x, i, axis):
        return lax.dynamic_index_in_dim(x, i, axis, keepdims=False)

    lower = lower_blocks[:, :, 0]
    slot = jnp.arange(lower.shape[2], dtype=jnp.int32)
    active = slot[None, None, :] < row_counts
    lower = jnp.where(active[..., None, None], lower, jnp.zeros((), bf16))
    lower = lower.reshape(lower.shape[:2] + (3, 2, chunk, block))

    def rows_of(level, e):
        k = me ^ e
        rows = [dyn(inverse_blocks[level, :, 0], k, 0), dyn(right_sides[level, :, 0], k, 0)]
        if level + 1 < levels:
            mine = dyn(lower[level], k, 0)
            rows.append(dyn(mine, core, 1).reshape(3 * chunk, block))
            rows.append(dyn(mine, 1 - core, 1).reshape(3 * chunk, block))
        return rows

    data = {}
    for batch in BATCHES:
        got = exchanged(lambda e: jnp.concatenate(sum([rows_of(level, e) for level in batch], [])))
        at = 0
        own, send = [], []
        for level in batch:
            inv = in_order(got[:, at : at + chunk]).reshape(block, block)
            at += chunk
            right = got[:, at : at + part].reshape(4 * part, block)
            at += part
            pieces = [inv, right]
            if level + 1 < levels:
                for _ in range(2):
                    low = in_order(got[:, at : at + 3 * chunk]).reshape(4, 3, chunk, block)
                    pieces.append(low.transpose(1, 0, 2, 3).reshape(3 * block, block))
                    at += 3 * chunk
                send += [inv, right, pieces[3]]
            else:
                send += [inv, right]
            own.append(pieces)
        other = to_core(jnp.concatenate(send))
        at = 0
        for level, pieces in zip(batch, own):
            inv = jnp.stack([pieces[0], other[at : at + block]])
            at += block
            right = jnp.stack([pieces[1], other[at : at + 4 * part]])
            at += 4 * part
            low = None
            if level + 1 < levels:
                low = jnp.stack([pieces[2], other[at : at + 3 * block]]).reshape(2, 3, block, block)
                at += 3 * block
            data[level] = (inv, right, low)

    incoming = None
    solved_levels = []
    for level in range(levels):
        inv, right, low = data[level]
        rest = right if incoming is None else (right.astype(f32) - incoming).astype(bf16)
        solved = jnp.einsum("prj,pij->pri", rest, inv, preferred_element_type=f32).astype(bf16)
        solved_levels.append(solved[0])
        if level + 1 < levels:
            updates = jnp.einsum("prj,pmij->pmri", solved, low, preferred_element_type=f32)
            far = to_next(updates[1, 2].astype(bf16), 2)
            near = jnp.stack([updates[0, 1] + updates[1, 0], updates[0, 2] + updates[1, 1]])
            near = to_next(near.astype(bf16), 1).astype(f32)
            mine = jnp.stack([near[0] + far.astype(f32), near[1] + updates[0, 0]]).astype(bf16)
            theirs = to_core(mine)
            incoming = mine.astype(f32) + theirs[::-1].astype(f32)

    out = jnp.stack(solved_levels).reshape(levels, 4, part, block)
    out = exchanged(lambda e: dyn(out, jnp.asarray(e), 1))
    return in_order(out).transpose(1, 0, 2, 3)[:, :, None]


def solution(mesh):
    n_blk = mesh.shape["blk"]
    return jax.shard_map(
        lambda *args: local(n_blk, *args),
        mesh=mesh,
        in_specs=(
            P(None, None, "blk", "rhs", None),
            P(None, None, "blk", "rhs", None),
            P(None, None, "blk", None, "rhs", None),
            P(None, None, "blk"),
        ),
        out_specs=P(None, None, "blk", "rhs", None),
        check_vma=False,
    )
```

time: 220 us -> 146 us (0.66)
  the two profiles are of different devices: /device:TPU:16 before, /device:TPU:1 now
where the time goes in v1:
time: 146 us; the launch traced here: 145 us
  starting transfers between devices  60 us (41%)
  waiting for transfers between devices  53.4 us (37%)
  local copies, waits for them, and re-layouts  16.9 us (12%)
  other arithmetic  9.07 us (6%)
  matrix products  3.88 us (3%)
  between operations  1.62 us (1%)
    ppermute x20, starting transfers between devices, routed(): return lax.ppermute(x, AXES, pairs)  60 us
    ppermute x20, waiting for transfers between devices, routed(): return lax.ppermute(x, AXES, pairs)  53.4 us
    unnamed x82, local copies, waits for them, and re-layouts  7.96 us
  transfers between devices with their start and end apart: 20, of which 13 were waited for; matrix products, arithmetic and copies ran while one was open for 14% of the time, Pallas kernels for 0%

profile of v1, /device:TPU:1, one launch (start us, length us, event | category | flops | bytes accessed | tf_op | source)
XLA Modules:
  0.0 144.9 jit_solution(10548764144202487335)
XLA Ops:
  0.8 1.9 %bitcast_select_fusion = bf16[3,4,6,64,256]{4,3,2,1,0:T(8,128)(2,1)S(1)} fusion(bf16[3,4,1,6,64,256]{5,4,3,2,1,0:T(8,128)(2,1)} %param.6, pred[3,4,6]{2,1,0:T(4,128)(4,1)S(1)} %iota_compare_fusion), kind=kLoop, calls=%fused_computation | loop fusion | flops 1179648 | bytes 4718664 | tf_op jit(solution)/shard_map/jit(_where)/select_n | solution.py:57
  2.8 0.9 copy-done.12
  4.2 5.5 %collective-permute-start = (bf16[2,528,256]{2,1,0:T(8,128)(2,1)S(1)}, bf16[2,528,256]{2,1,0:T(8,128)(2,1)S(1)}, u32[]{:S(2)}, u32[]{:S(2)}) collective-permute-start(bf16[2,528,256]{2,1,0:T(8,128)(2,1)S(1)} %pad_maximum_fusion.6), channel_id=1, source_target_pairs={{0,1},{1,0},{2,3},{3,2},{4,7},{5,6},{6,5},{7,4},{8,9},{9,8},{10,11... | collective-permute-start | bytes 1622024 | tf_op jit(solution)/shard_map/ppermute | solution.py:26
  10.0 0.8 pad_maximum_fusion.8
  10.8 1.9 %collective-permute-start.3 = (bf16[2,528,256]{2,1,0:T(8,128)(2,1)}, bf16[2,528,256]{2,1,0:T(8,128)(2,1)}, u32[]{:S(2)}, u32[]{:S(2)}) collective-permute-start(bf16[2,528,256]{2,1,0:T(8,128)(2,1)} %pad_maximum_fusion.8), channel_id=1, source_target_pairs={{0,1},{1,0},{2,3},{3,2},{4,7},{5,6},{6,5},{7,4},{8,9},{9,8},{10,11... | collective-permute-start | bytes 1622024 | tf_op jit(solution)/shard_map/ppermute | solution.py:26
  13.1 4.6 %collective-permute-start.9 = (bf16[2,672,256]{2,1,0:T(8,128)(2,1)S(1)}, bf16[2,672,256]{2,1,0:T(8,128)(2,1)S(1)}, u32[]{:S(2)}, u32[]{:S(2)}) collective-permute-start(bf16[2,672,256]{2,1,0:T(8,128)(2,1)S(1)} %pad_maximum_fusion.3), channel_id=1, source_target_pairs={{0,1},{1,0},{2,3},{3,2},{4,7},{5,6},{6,5},{7,4},{8,9},{9,8},{10,11... | collective-permute-start | bytes 2064392 | tf_op jit(solution)/shard_map/ppermute | solution.py:26
  17.7 0.7 fusion.98
  19.7 0.8 copy-done.19
  20.5 0.9 pad_maximum_fusion.7
  21.4 1.9 %collective-permute-start.1 = (bf16[2,528,256]{2,1,0:T(8,128)(2,1)}, bf16[2,528,256]{2,1,0:T(8,128)(2,1)S(1)}, u32[]{:S(2)}, u32[]{:S(2)}) collective-permute-start(bf16[2,528,256]{2,1,0:T(8,128)(2,1)} %pad_maximum_fusion.7), channel_id=1, source_target_pairs={{0,3},{1,2},{2,1},{3,0},{4,5},{5,4},{6,7},{7,6},{8,11},{9,10},{10,... | collective-permute-start | bytes 1622024 | tf_op jit(solution)/shard_map/ppermute | solution.py:26
  24.0 1.0 slice.729
  25.1 3.4 %collective-permute-start.4 = (bf16[2,528,256]{2,1,0:T(8,128)(2,1)S(1)}, bf16[2,528,256]{2,1,0:T(8,128)(2,1)S(1)}, u32[]{:S(2)}, u32[]{:S(2)}) collective-permute-start(bf16[2,528,256]{2,1,0:T(8,128)(2,1)S(1)} %pad_maximum_fusion.9), channel_id=1, source_target_pairs={{0,3},{1,2},{2,1},{3,0},{4,5},{5,4},{6,7},{7,6},{8,11},{9,10},{10,... | collective-permute-start | bytes 1622024 | tf_op jit(solution)/shard_map/ppermute | solution.py:26
  28.5 3.0 %collective-permute-done.9 = bf16[2,672,256]{2,1,0:T(8,128)(2,1)S(1)} collective-permute-done((bf16[2,672,256]{2,1,0:T(8,128)(2,1)S(1)}, bf16[2,672,256]{2,1,0:T(8,128)(2,1)S(1)}, u32[]{:S(2)}, u32[]{:S(2)}) %collective-permute-start.9) | collective-permute-done | bytes 688160 | tf_op jit(solution)/shard_map/ppermute | solution.py:26
  31.5 1.9 %collective-permute-start.10 = (bf16[2,672,256]{2,1,0:T(8,128)(2,1)S(1)}, bf16[2,672,256]{2,1,0:T(8,128)(2,1)S(1)}, u32[]{:S(2)}, u32[]{:S(2)}) collective-permute-start(bf16[2,672,256]{2,1,0:T(8,128)(2,1)S(1)} %pad_maximum_fusion.4), channel_id=1, source_target_pairs={{0,3},{1,2},{2,1},{3,0},{4,5},{5,4},{6,7},{7,6},{8,11},{9,10},{10,... | collective-permute-start | bytes 2064392 | tf_op jit(solution)/shard_map/ppermute | solution.py:26
  33.5 4.3 %collective-permute-done.1 = bf16[2,528,256]{2,1,0:T(8,128)(2,1)S(1)} collective-permute-done((bf16[2,528,256]{2,1,0:T(8,128)(2,1)}, bf16[2,528,256]{2,1,0:T(8,128)(2,1)S(1)}, u32[]{:S(2)}, u32[]{:S(2)}) %collective-permute-start.1) | collective-permute-done | bytes 540704 | tf_op jit(solution)/shard_map/ppermute | solution.py:26
  37.9 8.4 %collective-permute-done.4 = bf16[2,528,256]{2,1,0:T(8,128)(2,1)S(1)} collective-permute-done((bf16[2,528,256]{2,1,0:T(8,128)(2,1)S(1)}, bf16[2,528,256]{2,1,0:T(8,128)(2,1)S(1)}, u32[]{:S(2)}, u32[]{:S(2)}) %collective-permute-start.4) | collective-permute-done | bytes 540704 | tf_op jit(solution)/shard_map/ppermute | solution.py:26
  46.4 1.0 broadcast_select_fusion.3
  47.6 0.7 copy-done.28
  48.9 2.1 %collective-permute-start.2 = (bf16[1344,256]{1,0:T(8,128)(2,1)S(1)}, bf16[1344,256]{1,0:T(8,128)(2,1)S(1)}, u32[]{:S(2)}, u32[]{:S(2)}) collective-permute-start(bf16[1344,256]{1,0:T(8,128)(2,1)S(1)} %pad_maximum_fusion.1), channel_id=1, source_target_pairs={{0,4},{1,5},{2,6},{3,7},{4,0},{5,1},{6,2},{7,3},{8,12},{9,13},{10,... | collective-permute-start | bytes 2064392 | tf_op jit(solution)/shard_map/ppermute | solution.py:26
  51.3 0.7 copy-done.27
  52.5 2.2 %collective-permute-start.5 = (bf16[1344,256]{1,0:T(8,128)(2,1)S(1)}, bf16[1344,256]{1,0:T(8,128)(2,1)S(1)}, u32[]{:S(2)}, u32[]{:S(2)}) collective-permute-start(bf16[1344,256]{1,0:T(8,128)(2,1)S(1)} %pad_maximum_fusion.2), channel_id=1, source_target_pairs={{0,4},{1,5},{2,6},{3,7},{4,0},{5,1},{6,2},{7,3},{8,12},{9,13},{10,... | collective-permute-start | bytes 2064392 | tf_op jit(solution)/shard_map/ppermute | solution.py:26
  56.3 0.7 constant_dynamic-update-slice_fusion.28
  57.7 0.8 constant_dynamic-update-slice_fusion.26
  58.5 0.7 constant_dynamic-update-slice_fusion.25
  60.4 8.4 %collective-permute-start.6 = (bf16[2,320,256]{2,1,0:T(8,128)(2,1)S(1)}, bf16[2,320,256]{2,1,0:T(8,128)(2,1)S(1)}, u32[]{:S(2)}, u32[]{:S(2)}) collective-permute-start(bf16[2,320,256]{2,1,0:T(8,128)(2,1)S(1)} %pad_maximum_fusion.16), channel_id=1, source_target_pairs={{0,8},{1,9},{2,10},{3,11},{4,508},{5,509},{6,510},{7,511},{8,16},{... | collective-permute-start | bytes 983048 | tf_op jit(solution)/shard_map/ppermute | solution.py:26
  68.8 2.4 %collective-permute-start.7 = (bf16[320,256]{1,0:T(8,128)(2,1)S(1)}, bf16[320,256]{1,0:T(8,128)(2,1)S(1)}, u32[]{:S(2)}, u32[]{:S(2)}) collective-permute-start(bf16[320,256]{1,0:T(8,128)(2,1)S(1)} %fusion.61), channel_id=1, source_target_pairs={{0,16},{1,17},{2,18},{3,19},{4,500},{5,501},{6,502},{7,503},{8,24}... | collective-permute-start | bytes 491528 | tf_op jit(solution)/shard_map/ppermute | solution.py:26
  72.0 1.9 %collective-permute-start.11 = (bf16[1920,256]{1,0:T(8,128)(2,1)}, bf16[1920,256]{1,0:T(8,128)(2,1)S(1)}, u32[]{:S(2)}, u32[]{:S(2)}) collective-permute-start(bf16[1920,256]{1,0:T(8,128)(2,1)} %constant_dynamic-update-slice_fusion.24), channel_id=1, source_target_pairs={{0,4},{1,5},{2,6},{3,7},{4,0},{5,1},{6,2},{7,3},{8,12},{9,13},{10,... | collective-permute-start | bytes 2949128 | tf_op jit(solution)/shard_map/ppermute | solution.py:26
  74.1 5.0 %collective-permute-done.7 = bf16[320,256]{1,0:T(8,128)(2,1)S(1)} collective-permute-done((bf16[320,256]{1,0:T(8,128)(2,1)S(1)}, bf16[320,256]{1,0:T(8,128)(2,1)S(1)}, u32[]{:S(2)}, u32[]{:S(2)}) %collective-permute-start.7) | collective-permute-done | bytes 163872 | tf_op jit(solution)/shard_map/ppermute | solution.py:26
  79.2 1.9 %collective-permute-start.8 = (bf16[2,320,256]{2,1,0:T(8,128)(2,1)S(1)}, bf16[2,320,256]{2,1,0:T(8,128)(2,1)}, u32[]{:S(2)}, u32[]{:S(2)}) collective-permute-start(bf16[2,320,256]{2,1,0:T(8,128)(2,1)S(1)} %pad_maximum_fusion.17), channel_id=1, source_target_pairs={{0,4},{1,5},{2,6},{3,7},{4,0},{5,1},{6,2},{7,3},{8,12},{9,13},{10,... | collective-permute-start | bytes 983048 | tf_op jit(solution)/shard_map/ppermute | solution.py:26
  82.9 1.7 %rev.9 = bf16[2,320,256]{2,1,0:T(8,128)(2,1)} reverse(bf16[2,320,256]{2,1,0:T(8,128)(2,1)} %collective-permute-done.8), dimensions={0} | reverse | bytes 655360 | tf_op jit(solution)/shard_map/rev | solution.py:116
  84.6 1.6 %convolution_convert_fusion.1 = bf16[2,320,256]{2,1,0:T(8,128)(2,1)S(1)} fusion(bf16[2,320,256]{2,1,0:T(8,128)(2,1)} %rev.9, bf16[1,320,256]{2,1,0:T(8,128)(2,1)} %slice_bitcast_fusion.10, bf16[1,320,256]{2,1,0:T(8,128)(2,1)} %bitcast.306, bf16[1,256,256]{2,1,0:T(8,128)(2,1)} %slice_bitcast_fusion.14, bf16[1,256,256]{2,1,0:T(8,128)(2,1)} %bitcast.318, ...), kind=kOutput, calls=%fused_computation.6 | convolution fusion | flops 85491712 | bytes 1572864 | tf_op jit(solution)/shard_map/prj,pij->pri/dot_general | solution.py:107
  87.0 4.7 %collective-permute-start.12 = (bf16[2,320,256]{2,1,0:T(8,128)(2,1)S(1)}, bf16[2,320,256]{2,1,0:T(8,128)(2,1)S(1)}, u32[]{:S(2)}, u32[]{:S(2)}) collective-permute-start(bf16[2,320,256]{2,1,0:T(8,128)(2,1)S(1)} %pad_maximum_fusion.18), channel_id=1, source_target_pairs={{0,8},{1,9},{2,10},{3,11},{4,508},{5,509},{6,510},{7,511},{8,16},{... | collective-permute-start | bytes 983048 | tf_op jit(solution)/shard_map/ppermute | solution.py:26
  91.7 1.9 %collective-permute-start.13 = (bf16[320,256]{1,0:T(8,128)(2,1)S(1)}, bf16[320,256]{1,0:T(8,128)(2,1)S(1)}, u32[]{:S(2)}, u32[]{:S(2)}) collective-permute-start(bf16[320,256]{1,0:T(8,128)(2,1)S(1)} %fusion.65), channel_id=1, source_target_pairs={{0,16},{1,17},{2,18},{3,19},{4,500},{5,501},{6,502},{7,503},{8,24}... | collective-permute-start | bytes 491528 | tf_op jit(solution)/shard_map/ppermute | solution.py:26
  93.9 4.7 %collective-permute-done.12 = bf16[2,320,256]{2,1,0:T(8,128)(2,1)S(1)} collective-permute-done((bf16[2,320,256]{2,1,0:T(8,128)(2,1)S(1)}, bf16[2,320,256]{2,1,0:T(8,128)(2,1)S(1)}, u32[]{:S(2)}, u32[]{:S(2)}) %collective-permute-start.12) | collective-permute-done | bytes 327712 | tf_op jit(solution)/shard_map/ppermute | solution.py:26
  98.7 3.6 %collective-permute-done.13 = bf16[320,256]{1,0:T(8,128)(2,1)S(1)} collective-permute-done((bf16[320,256]{1,0:T(8,128)(2,1)S(1)}, bf16[320,256]{1,0:T(8,128)(2,1)S(1)}, u32[]{:S(2)}, u32[]{:S(2)}) %collective-permute-start.13) | collective-permute-done | bytes 163872 | tf_op jit(solution)/shard_map/ppermute | solution.py:26
  102.5 2.1 %collective-permute-start.14 = (bf16[2,320,256]{2,1,0:T(8,128)(2,1)S(1)}, bf16[2,320,256]{2,1,0:T(8,128)(2,1)S(1)}, u32[]{:S(2)}, u32[]{:S(2)}) collective-permute-start(bf16[2,320,256]{2,1,0:T(8,128)(2,1)S(1)} %pad_maximum_fusion.19), channel_id=1, source_target_pairs={{0,4},{1,5},{2,6},{3,7},{4,0},{5,1},{6,2},{7,3},{8,12},{9,13},{10,... | collective-permute-start | bytes 983048 | tf_op jit(solution)/shard_map/ppermute | solution.py:26
  104.6 1.5 %collective-permute-done.14 = bf16[2,320,256]{2,1,0:T(8,128)(2,1)S(1)} collective-permute-done((bf16[2,320,256]{2,1,0:T(8,128)(2,1)S(1)}, bf16[2,320,256]{2,1,0:T(8,128)(2,1)S(1)}, u32[]{:S(2)}, u32[]{:S(2)}) %collective-permute-start.14) | collective-permute-done | bytes 327712 | tf_op jit(solution)/shard_map/ppermute | solution.py:26
  107.0 4.4 %collective-permute-start.15 = (bf16[2,320,256]{2,1,0:T(8,128)(2,1)S(1)}, bf16[2,320,256]{2,1,0:T(8,128)(2,1)S(1)}, u32[]{:S(2)}, u32[]{:S(2)}) collective-permute-start(bf16[2,320,256]{2,1,0:T(8,128)(2,1)S(1)} %pad_maximum_fusion.20), channel_id=1, source_target_pairs={{0,8},{1,9},{2,10},{3,11},{4,508},{5,509},{6,510},{7,511},{8,16},{... | collective-permute-start | bytes 983048 | tf_op jit(solution)/shard_map/ppermute | solution.py:26
  111.5 1.9 %collective-permute-start.16 = (bf16[320,256]{1,0:T(8,128)(2,1)S(1)}, bf16[320,256]{1,0:T(8,128)(2,1)S(1)}, u32[]{:S(2)}, u32[]{:S(2)}) collective-permute-start(bf16[320,256]{1,0:T(8,128)(2,1)S(1)} %fusion.69), channel_id=1, source_target_pairs={{0,16},{1,17},{2,18},{3,19},{4,500},{5,501},{6,502},{7,503},{8,24}... | collective-permute-start | bytes 491528 | tf_op jit(solution)/shard_map/ppermute | solution.py:26
  113.4 5.3 %collective-permute-done.15 = bf16[2,320,256]{2,1,0:T(8,128)(2,1)S(1)} collective-permute-done((bf16[2,320,256]{2,1,0:T(8,128)(2,1)S(1)}, bf16[2,320,256]{2,1,0:T(8,128)(2,1)S(1)}, u32[]{:S(2)}, u32[]{:S(2)}) %collective-permute-start.15) | collective-permute-done | bytes 327712 | tf_op jit(solution)/shard_map/ppermute | solution.py:26
  118.8 3.5 %collective-permute-done.16 = bf16[320,256]{1,0:T(8,128)(2,1)S(1)} collective-permute-done((bf16[320,256]{1,0:T(8,128)(2,1)S(1)}, bf16[320,256]{1,0:T(8,128)(2,1)S(1)}, u32[]{:S(2)}, u32[]{:S(2)}) %collective-permute-start.16) | collective-permute-done | bytes 163872 | tf_op jit(solution)/shard_map/ppermute | solution.py:26
  122.4 1.9 %collective-permute-start.17 = (bf16[2,320,256]{2,1,0:T(8,128)(2,1)S(1)}, bf16[2,320,256]{2,1,0:T(8,128)(2,1)S(1)}, u32[]{:S(2)}, u32[]{:S(2)}) collective-permute-start(bf16[2,320,256]{2,1,0:T(8,128)(2,1)S(1)} %pad_maximum_fusion.21), channel_id=1, source_target_pairs={{0,4},{1,5},{2,6},{3,7},{4,0},{5,1},{6,2},{7,3},{8,12},{9,13},{10,... | collective-permute-start | bytes 983048 | tf_op jit(solution)/shard_map/ppermute | solution.py:26
  124.4 1.6 %collective-permute-done.17 = bf16[2,320,256]{2,1,0:T(8,128)(2,1)S(1)} collective-permute-done((bf16[2,320,256]{2,1,0:T(8,128)(2,1)S(1)}, bf16[2,320,256]{2,1,0:T(8,128)(2,1)S(1)}, u32[]{:S(2)}, u32[]{:S(2)}) %collective-permute-start.17) | collective-permute-done | bytes 327712 | tf_op jit(solution)/shard_map/ppermute | solution.py:26
  126.5 3.0 %collective-permute-start.18 = (bf16[2,4,80,256]{3,2,0,1:T(8,128)(2,1)S(1)}, bf16[2,4,80,256]{3,2,0,1:T(8,128)(2,1)S(1)}, u32[]{:S(2)}, u32[]{:S(2)}) collective-permute-start(bf16[2,4,80,256]{3,2,0,1:T(8,128)(2,1)S(1)} %pad_maximum_fusion.22), channel_id=1, source_target_pairs={{0,1},{1,0},{2,3},{3,2},{4,7},{5,6},{6,5},{7,4},{8,9},{9,8},{10,11... | collective-permute-start | bytes 983048 | tf_op jit(solution)/shard_map/ppermute | solution.py:26
  129.5 6.0 %collective-permute-done.18 = bf16[2,4,80,256]{3,2,0,1:T(8,128)(2,1)S(1)} collective-permute-done((bf16[2,4,80,256]{3,2,0,1:T(8,128)(2,1)S(1)}, bf16[2,4,80,256]{3,2,0,1:T(8,128)(2,1)S(1)}, u32[]{:S(2)}, u32[]{:S(2)}) %collective-permute-start.18) | collective-permute-done | bytes 327712 | tf_op jit(solution)/shard_map/ppermute | solution.py:26
  135.6 1.9 %collective-permute-start.19 = (bf16[2,4,80,256]{3,2,0,1:T(8,128)(2,1)S(1)}, bf16[2,4,80,256]{3,2,0,1:T(8,128)(2,1)S(1)}, u32[]{:S(2)}, u32[]{:S(2)}) collective-permute-start(bf16[2,4,80,256]{3,2,0,1:T(8,128)(2,1)S(1)} %pad_maximum_fusion.23), channel_id=1, source_target_pairs={{0,3},{1,2},{2,1},{3,0},{4,5},{5,4},{6,7},{7,6},{8,11},{9,10},{10,... | collective-permute-start | bytes 983048 | tf_op jit(solution)/shard_map/ppermute | solution.py:26
  137.5 6.2 %collective-permute-done.19 = bf16[2,4,80,256]{3,2,0,1:T(8,128)(2,1)S(1)} collective-permute-done((bf16[2,4,80,256]{3,2,0,1:T(8,128)(2,1)S(1)}, bf16[2,4,80,256]{3,2,0,1:T(8,128)(2,1)S(1)}, u32[]{:S(2)}, u32[]{:S(2)}) %collective-permute-start.19) | collective-permute-done | bytes 327712 | tf_op jit(solution)/shard_map/ppermute | solution.py:26
  143.9 1.0 fusion.9
  (224 shorter events, 14.2 us)
Async XLA Ops:
  2.7 1.1 copy-start.12
  2.7 1.2 copy-start.21
  4.2 15.5 %collective-permute-start = (bf16[2,528,256]{2,1,0:T(8,128)(2,1)S(1)}, bf16[2,528,256]{2,1,0:T(8,128)(2,1)S(1)}, u32[]{:S(2)}, u32[]{:S(2)}) collective-permute-start(bf16[2,528,256]{2,1,0:T(8,128)(2,1)S(1)} %pad_maximum_fusion.6), channel_id=1, source_target_pairs={{0,1},{1,0},{2,3},{3,2},{4,7},{5,6},{6,5},{7,4},{8,9},{9,8},{10,11... | collective-permute-start | bytes 1622024 | tf_op jit(solution)/shard_map/ppermute | solution.py:26
  10.8 13.2 %collective-permute-start.3 = (bf16[2,528,256]{2,1,0:T(8,128)(2,1)}, bf16[2,528,256]{2,1,0:T(8,128)(2,1)}, u32[]{:S(2)}, u32[]{:S(2)}) collective-permute-start(bf16[2,528,256]{2,1,0:T(8,128)(2,1)} %pad_maximum_fusion.8), channel_id=1, source_target_pairs={{0,1},{1,0},{2,3},{3,2},{4,7},{5,6},{6,5},{7,4},{8,9},{9,8},{10,11... | collective-permute-start | bytes 1622024 | tf_op jit(solution)/shard_map/ppermute | solution.py:26
  13.1 18.3 %collective-permute-start.9 = (bf16[2,672,256]{2,1,0:T(8,128)(2,1)S(1)}, bf16[2,672,256]{2,1,0:T(8,128)(2,1)S(1)}, u32[]{:S(2)}, u32[]{:S(2)}) collective-permute-start(bf16[2,672,256]{2,1,0:T(8,128)(2,1)S(1)} %pad_maximum_fusion.3), channel_id=1, source_target_pairs={{0,1},{1,0},{2,3},{3,2},{4,7},{5,6},{6,5},{7,4},{8,9},{9,8},{10,11... | collective-permute-start | bytes 2064392 | tf_op jit(solution)/shard_map/ppermute | solution.py:26
  21.4 16.4 %collective-permute-start.1 = (bf16[2,528,256]{2,1,0:T(8,128)(2,1)}, bf16[2,528,256]{2,1,0:T(8,128)(2,1)S(1)}, u32[]{:S(2)}, u32[]{:S(2)}) collective-permute-start(bf16[2,528,256]{2,1,0:T(8,128)(2,1)} %pad_maximum_fusion.7), channel_id=1, source_target_pairs={{0,3},{1,2},{2,1},{3,0},{4,5},{5,4},{6,7},{7,6},{8,11},{9,10},{10,... | collective-permute-start | bytes 1622024 | tf_op jit(solution)/shard_map/ppermute | solution.py:26
  24.0 13.8 %copy-start.20 = (bf16[2,528,256]{2,1,0:T(8,128)(2,1)S(1)}, bf16[2,528,256]{2,1,0:T(8,128)(2,1)}, u32[]{:S(2)}) copy-start(bf16[2,528,256]{2,1,0:T(8,128)(2,1)} %copy-done.19) | copy-start | bytes 1622020
  24.0 49.9 %copy-start = (bf16[1,192,256]{2,1,0:T(8,128)(2,1)}, bf16[1,192,256]{2,1,0:T(8,128)(2,1)S(1)}, u32[]{:S(2)}) copy-start(bf16[1,192,256]{2,1,0:T(8,128)(2,1)S(1)} %get-tuple-element.97) | copy-start | bytes 294916
  25.1 21.3 %collective-permute-start.4 = (bf16[2,528,256]{2,1,0:T(8,128)(2,1)S(1)}, bf16[2,528,256]{2,1,0:T(8,128)(2,1)S(1)}, u32[]{:S(2)}, u32[]{:S(2)}) collective-permute-start(bf16[2,528,256]{2,1,0:T(8,128)(2,1)S(1)} %pad_maximum_fusion.9), channel_id=1, source_target_pairs={{0,3},{1,2},{2,1},{3,0},{4,5},{5,4},{6,7},{7,6},{8,11},{9,10},{10,... | collective-permute-start | bytes 1622024 | tf_op jit(solution)/shard_map/ppermute | solution.py:26
  31.5 23.4 %collective-permute-start.10 = (bf16[2,672,256]{2,1,0:T(8,128)(2,1)S(1)}, bf16[2,672,256]{2,1,0:T(8,128)(2,1)S(1)}, u32[]{:S(2)}, u32[]{:S(2)}) collective-permute-start(bf16[2,672,256]{2,1,0:T(8,128)(2,1)S(1)} %pad_maximum_fusion.4), channel_id=1, source_target_pairs={{0,3},{1,2},{2,1},{3,0},{4,5},{5,4},{6,7},{7,6},{8,11},{9,10},{10,... | collective-permute-start | bytes 2064392 | tf_op jit(solution)/shard_map/ppermute | solution.py:26
  37.9 9.6 %copy-start.30 = (bf16[1,64,256]{2,1,0:T(8,128)(2,1)S(1)}, bf16[1,64,256]{2,1,0:T(8,128)(2,1)}, u32[]{:S(2)}) copy-start(bf16[1,64,256]{2,1,0:T(8,128)(2,1)} %slice.713) | copy-start | bytes 98308
  47.4 0.9 copy-start.29
  48.9 10.4 %collective-permute-start.2 = (bf16[1344,256]{1,0:T(8,128)(2,1)S(1)}, bf16[1344,256]{1,0:T(8,128)(2,1)S(1)}, u32[]{:S(2)}, u32[]{:S(2)}) collective-permute-start(bf16[1344,256]{1,0:T(8,128)(2,1)S(1)} %pad_maximum_fusion.1), channel_id=1, source_target_pairs={{0,4},{1,5},{2,6},{3,7},{4,0},{5,1},{6,2},{7,3},{8,12},{9,13},{10,... | collective-permute-start | bytes 2064392 | tf_op jit(solution)/shard_map/ppermute | solution.py:26
  51.2 1.3 copy-start.14
  52.4 2.4 %copy-start.26 = (bf16[4,64,256]{2,1,0:T(8,128)(2,1)}, bf16[4,64,256]{2,1,0:T(8,128)(2,1)S(1)}, u32[]{:S(2)}) copy-start(bf16[4,64,256]{2,1,0:T(8,128)(2,1)S(1)} %maximum_select_fusion.16) | copy-start | bytes 393220
  52.5 28.7 %collective-permute-start.5 = (bf16[1344,256]{1,0:T(8,128)(2,1)S(1)}, bf16[1344,256]{1,0:T(8,128)(2,1)S(1)}, u32[]{:S(2)}, u32[]{:S(2)}) collective-permute-start(bf16[1344,256]{1,0:T(8,128)(2,1)S(1)} %pad_maximum_fusion.2), channel_id=1, source_target_pairs={{0,4},{1,5},{2,6},{3,7},{4,0},{5,1},{6,2},{7,3},{8,12},{9,13},{10,... | collective-permute-start | bytes 2064392 | tf_op jit(solution)/shard_map/ppermute | solution.py:26
  55.0 18.9 %copy-start.2 = (bf16[1,192,256]{2,1,0:T(8,128)(2,1)}, bf16[1,192,256]{2,1,0:T(8,128)(2,1)S(1)}, u32[]{:S(2)}) copy-start(bf16[1,192,256]{2,1,0:T(8,128)(2,1)S(1)} %get-tuple-element.99) | copy-start | bytes 294916
  55.0 18.8 %copy-start.4 = (bf16[1,192,256]{2,1,0:T(8,128)(2,1)}, bf16[1,192,256]{2,1,0:T(8,128)(2,1)S(1)}, u32[]{:S(2)}) copy-start(bf16[1,192,256]{2,1,0:T(8,128)(2,1)S(1)} %get-tuple-element.95) | copy-start | bytes 294916
  55.3 1.7 %copy-start.17 = (bf16[4,80,256]{2,1,0:T(8,128)(2,1)}, bf16[4,80,256]{2,1,0:T(8,128)(2,1)S(1)}, u32[]{:S(2)}) copy-start(bf16[4,80,256]{2,1,0:T(8,128)(2,1)S(1)} %get-tuple-element.15) | copy-start | bytes 491524
  55.3 16.0 %copy-start.15 = (bf16[4,80,256]{2,1,0:T(8,128)(2,1)}, bf16[4,80,256]{2,1,0:T(8,128)(2,1)S(1)}, u32[]{:S(2)}) copy-start(bf16[4,80,256]{2,1,0:T(8,128)(2,1)S(1)} %get-tuple-element.14) | copy-start | bytes 491524
  55.3 18.6 %copy-start.6 = (bf16[1,192,256]{2,1,0:T(8,128)(2,1)}, bf16[1,192,256]{2,1,0:T(8,128)(2,1)S(1)}, u32[]{:S(2)}) copy-start(bf16[1,192,256]{2,1,0:T(8,128)(2,1)S(1)} %get-tuple-element.56) | copy-start | bytes 294916
  56.3 3.0 %copy-start.24 = (bf16[4,64,256]{2,1,0:T(8,128)(2,1)}, bf16[4,64,256]{2,1,0:T(8,128)(2,1)S(1)}, u32[]{:S(2)}) copy-start(bf16[4,64,256]{2,1,0:T(8,128)(2,1)S(1)} %maximum_select_fusion.17) | copy-start | bytes 393220
  60.4 13.7 %collective-permute-start.6 = (bf16[2,320,256]{2,1,0:T(8,128)(2,1)S(1)}, bf16[2,320,256]{2,1,0:T(8,128)(2,1)S(1)}, u32[]{:S(2)}, u32[]{:S(2)}) collective-permute-start(bf16[2,320,256]{2,1,0:T(8,128)(2,1)S(1)} %pad_maximum_fusion.16), channel_id=1, source_target_pairs={{0,8},{1,9},{2,10},{3,11},{4,508},{5,509},{6,510},{7,511},{8,16},{... | collective-permute-start | bytes 983048 | tf_op jit(solution)/shard_map/ppermute | solution.py:26
  68.8 10.2 %collective-permute-start.7 = (bf16[320,256]{1,0:T(8,128)(2,1)S(1)}, bf16[320,256]{1,0:T(8,128)(2,1)S(1)}, u32[]{:S(2)}, u32[]{:S(2)}) collective-permute-start(bf16[320,256]{1,0:T(8,128)(2,1)S(1)} %fusion.61), channel_id=1, source_target_pairs={{0,16},{1,17},{2,18},{3,19},{4,500},{5,501},{6,502},{7,503},{8,24}... | collective-permute-start | bytes 491528 | tf_op jit(solution)/shard_map/ppermute | solution.py:26
  72.0 32.6 %collective-permute-start.11 = (bf16[1920,256]{1,0:T(8,128)(2,1)}, bf16[1920,256]{1,0:T(8,128)(2,1)S(1)}, u32[]{:S(2)}, u32[]{:S(2)}) collective-permute-start(bf16[1920,256]{1,0:T(8,128)(2,1)} %constant_dynamic-update-slice_fusion.24), channel_id=1, source_target_pairs={{0,4},{1,5},{2,6},{3,7},{4,0},{5,1},{6,2},{7,3},{8,12},{9,13},{10,... | collective-permute-start | bytes 2949128 | tf_op jit(solution)/shard_map/ppermute | solution.py:26
  79.1 3.4 %copy-start.11 = (bf16[1,320,256]{2,1,0:T(8,128)(2,1)}, bf16[1,320,256]{2,1,0:T(8,128)(2,1)S(1)}, u32[]{:S(2)}) copy-start(bf16[1,320,256]{2,1,0:T(8,128)(2,1)S(1)} %fusion.60) | copy-start | bytes 491524
  79.2 3.3 %copy-start.13 = (bf16[1,320,256]{2,1,0:T(8,128)(2,1)}, bf16[1,320,256]{2,1,0:T(8,128)(2,1)S(1)}, u32[]{:S(2)}) copy-start(bf16[1,320,256]{2,1,0:T(8,128)(2,1)S(1)} %fusion.26) | copy-start | bytes 491524
  79.2 3.7 %collective-permute-start.8 = (bf16[2,320,256]{2,1,0:T(8,128)(2,1)S(1)}, bf16[2,320,256]{2,1,0:T(8,128)(2,1)}, u32[]{:S(2)}, u32[]{:S(2)}) collective-permute-start(bf16[2,320,256]{2,1,0:T(8,128)(2,1)S(1)} %pad_maximum_fusion.17), channel_id=1, source_target_pairs={{0,4},{1,5},{2,6},{3,7},{4,0},{5,1},{6,2},{7,3},{8,12},{9,13},{10,... | collective-permute-start | bytes 983048 | tf_op jit(solution)/shard_map/ppermute | solution.py:26
  86.7 7.0 %copy-start.1 = (bf16[1,192,256]{2,1,0:T(8,128)(2,1)S(1)}, bf16[1,192,256]{2,1,0:T(8,128)(2,1)}, u32[]{:S(2)}) copy-start(bf16[1,192,256]{2,1,0:T(8,128)(2,1)} %copy-done) | copy-start | bytes 294916
  86.7 7.0 %copy-start.3 = (bf16[1,192,256]{2,1,0:T(8,128)(2,1)S(1)}, bf16[1,192,256]{2,1,0:T(8,128)(2,1)}, u32[]{:S(2)}) copy-start(bf16[1,192,256]{2,1,0:T(8,128)(2,1)} %copy-done.2) | copy-start | bytes 294916
  86.7 7.0 %copy-start.5 = (bf16[1,192,256]{2,1,0:T(8,128)(2,1)S(1)}, bf16[1,192,256]{2,1,0:T(8,128)(2,1)}, u32[]{:S(2)}) copy-start(bf16[1,192,256]{2,1,0:T(8,128)(2,1)} %copy-done.4) | copy-start | bytes 294916
  86.7 7.0 %copy-start.7 = (bf16[1,192,256]{2,1,0:T(8,128)(2,1)S(1)}, bf16[1,192,256]{2,1,0:T(8,128)(2,1)}, u32[]{:S(2)}) copy-start(bf16[1,192,256]{2,1,0:T(8,128)(2,1)} %copy-done.6) | copy-start | bytes 294916
  87.0 11.6 %collective-permute-start.12 = (bf16[2,320,256]{2,1,0:T(8,128)(2,1)S(1)}, bf16[2,320,256]{2,1,0:T(8,128)(2,1)S(1)}, u32[]{:S(2)}, u32[]{:S(2)}) collective-permute-start(bf16[2,320,256]{2,1,0:T(8,128)(2,1)S(1)} %pad_maximum_fusion.18), channel_id=1, source_target_pairs={{0,8},{1,9},{2,10},{3,11},{4,508},{5,509},{6,510},{7,511},{8,16},{... | collective-permute-start | bytes 983048 | tf_op jit(solution)/shard_map/ppermute | solution.py:26
  91.7 10.6 %collective-permute-start.13 = (bf16[320,256]{1,0:T(8,128)(2,1)S(1)}, bf16[320,256]{1,0:T(8,128)(2,1)S(1)}, u32[]{:S(2)}, u32[]{:S(2)}) collective-permute-start(bf16[320,256]{1,0:T(8,128)(2,1)S(1)} %fusion.65), channel_id=1, source_target_pairs={{0,16},{1,17},{2,18},{3,19},{4,500},{5,501},{6,502},{7,503},{8,24}... | collective-permute-start | bytes 491528 | tf_op jit(solution)/shard_map/ppermute | solution.py:26
  102.3 3.8 %copy-start.18 = (bf16[4,80,256]{2,1,0:T(8,128)(2,1)S(1)}, bf16[4,80,256]{2,1,0:T(8,128)(2,1)}, u32[]{:S(2)}) copy-start(bf16[4,80,256]{2,1,0:T(8,128)(2,1)} %copy-done.17) | copy-start | bytes 491524
  102.3 3.8 %copy-start.25 = (bf16[4,64,256]{2,1,0:T(8,128)(2,1)S(1)}, bf16[4,64,256]{2,1,0:T(8,128)(2,1)}, u32[]{:S(2)}) copy-start(bf16[4,64,256]{2,1,0:T(8,128)(2,1)} %copy-done.24) | copy-start | bytes 393220
  102.5 3.7 %collective-permute-start.14 = (bf16[2,320,256]{2,1,0:T(8,128)(2,1)S(1)}, bf16[2,320,256]{2,1,0:T(8,128)(2,1)S(1)}, u32[]{:S(2)}, u32[]{:S(2)}) collective-permute-start(bf16[2,320,256]{2,1,0:T(8,128)(2,1)S(1)} %pad_maximum_fusion.19), channel_id=1, source_target_pairs={{0,4},{1,5},{2,6},{3,7},{4,0},{5,1},{6,2},{7,3},{8,12},{9,13},{10,... | collective-permute-start | bytes 983048 | tf_op jit(solution)/shard_map/ppermute | solution.py:26
  106.5 17.9 %copy-start.10 = (bf16[2,320,256]{2,1,0:T(8,128)(2,1)}, bf16[2,320,256]{2,1,0:T(8,128)(2,1)S(1)}, u32[]{:S(2)}) copy-start(bf16[2,320,256]{2,1,0:T(8,128)(2,1)S(1)} %convolution_convert_fusion) | copy-start | bytes 983044
  107.0 11.6 %collective-permute-start.15 = (bf16[2,320,256]{2,1,0:T(8,128)(2,1)S(1)}, bf16[2,320,256]{2,1,0:T(8,128)(2,1)S(1)}, u32[]{:S(2)}, u32[]{:S(2)}) collective-permute-start(bf16[2,320,256]{2,1,0:T(8,128)(2,1)S(1)} %pad_maximum_fusion.20), channel_id=1, source_target_pairs={{0,8},{1,9},{2,10},{3,11},{4,508},{5,509},{6,510},{7,511},{8,16},{... | collective-permute-start | bytes 983048 | tf_op jit(solution)/shard_map/ppermute | solution.py:26
  111.5 10.8 %collective-permute-start.16 = (bf16[320,256]{1,0:T(8,128)(2,1)S(1)}, bf16[320,256]{1,0:T(8,128)(2,1)S(1)}, u32[]{:S(2)}, u32[]{:S(2)}) collective-permute-start(bf16[320,256]{1,0:T(8,128)(2,1)S(1)} %fusion.69), channel_id=1, source_target_pairs={{0,16},{1,17},{2,18},{3,19},{4,500},{5,501},{6,502},{7,503},{8,24}... | collective-permute-start | bytes 491528 | tf_op jit(solution)/shard_map/ppermute | solution.py:26
  118.7 7.2 %copy-start.16 = (bf16[4,80,256]{2,1,0:T(8,128)(2,1)S(1)}, bf16[4,80,256]{2,1,0:T(8,128)(2,1)}, u32[]{:S(2)}) copy-start(bf16[4,80,256]{2,1,0:T(8,128)(2,1)} %copy-done.15) | copy-start | bytes 491524
  118.7 7.2 %copy-start.23 = (bf16[4,64,256]{2,1,0:T(8,128)(2,1)S(1)}, bf16[4,64,256]{2,1,0:T(8,128)(2,1)}, u32[]{:S(2)}) copy-start(bf16[4,64,256]{2,1,0:T(8,128)(2,1)} %copy-done.22) | copy-start | bytes 393220
  122.4 3.5 %collective-permute-start.17 = (bf16[2,320,256]{2,1,0:T(8,128)(2,1)S(1)}, bf16[2,320,256]{2,1,0:T(8,128)(2,1)S(1)}, u32[]{:S(2)}, u32[]{:S(2)}) collective-permute-start(bf16[2,320,256]{2,1,0:T(8,128)(2,1)S(1)} %pad_maximum_fusion.21), channel_id=1, source_target_pairs={{0,4},{1,5},{2,6},{3,7},{4,0},{5,1},{6,2},{7,3},{8,12},{9,13},{10,... | collective-permute-start | bytes 983048 | tf_op jit(solution)/shard_map/ppermute | solution.py:26
  124.3 2.0 %slice-start = ((bf16[2,320,256]{2,1,0:T(8,128)(2,1)}), bf16[1,320,256]{2,1,0:T(8,128)(2,1)S(1)}, s32[]{:S(2)}) async-start(bf16[2,320,256]{2,1,0:T(8,128)(2,1)} %copy-done.8), calls=%async_computation | async-start | bytes 327680 | tf_op jit(solution)/shard_map/slice | solution.py:108
  124.3 2.0 %slice-start.1 = ((bf16[2,320,256]{2,1,0:T(8,128)(2,1)}), bf16[1,320,256]{2,1,0:T(8,128)(2,1)S(1)}, s32[]{:S(2)}) async-start(bf16[2,320,256]{2,1,0:T(8,128)(2,1)} %copy-done.9), calls=%async_computation.1 | async-start | bytes 327680 | tf_op jit(solution)/shard_map/slice | solution.py:108
  124.3 2.0 %slice-start.2 = ((bf16[2,320,256]{2,1,0:T(8,128)(2,1)}), bf16[1,320,256]{2,1,0:T(8,128)(2,1)S(1)}, s32[]{:S(2)}) async-start(bf16[2,320,256]{2,1,0:T(8,128)(2,1)} %copy-done.10), calls=%async_computation.2 | async-start | bytes 327680 | tf_op jit(solution)/shard_map/slice | solution.py:108
  126.5 9.0 %collective-permute-start.18 = (bf16[2,4,80,256]{3,2,0,1:T(8,128)(2,1)S(1)}, bf16[2,4,80,256]{3,2,0,1:T(8,128)(2,1)S(1)}, u32[]{:S(2)}, u32[]{:S(2)}) collective-permute-start(bf16[2,4,80,256]{3,2,0,1:T(8,128)(2,1)S(1)} %pad_maximum_fusion.22), channel_id=1, source_target_pairs={{0,1},{1,0},{2,3},{3,2},{4,7},{5,6},{6,5},{7,4},{8,9},{9,8},{10,11... | collective-permute-start | bytes 983048 | tf_op jit(solution)/shard_map/ppermute | solution.py:26
  135.6 8.1 %collective-permute-start.19 = (bf16[2,4,80,256]{3,2,0,1:T(8,128)(2,1)S(1)}, bf16[2,4,80,256]{3,2,0,1:T(8,128)(2,1)S(1)}, u32[]{:S(2)}, u32[]{:S(2)}) collective-permute-start(bf16[2,4,80,256]{3,2,0,1:T(8,128)(2,1)S(1)} %pad_maximum_fusion.23), channel_id=1, source_target_pairs={{0,3},{1,2},{2,1},{3,0},{4,5},{5,4},{6,7},{7,6},{8,11},{9,10},{10,... | collective-permute-start | bytes 983048 | tf_op jit(solution)/shard_map/ppermute | solution.py:26
  (8 other events, 6.5 us)
